TPU v7x, 512 devices: a whole 4x8x8 slice. The times are simulated.
512 devices in a mesh: mem: 2 (over core), tile: 256 (over z, y, x).
Axes of the slice: x: 4, y: 8, z: 8, core: 2. Of those that a mesh axis runs over, the one named last changes fastest.
Arguments:
- anomalies: bfloat16 [1024, 256, 512], P('tile', 'mem'), may hold values from -6 to 6
- innovations: bfloat16 [2048, 256, 512], P('tile', 'mem'), may hold values from -3 to 3
- obs_tile: int32 [2048], P('tile'), may hold values from 0 to 1023, as said below
- pair_tiles: int32 [2048, 2], P('tile'), may hold values from 0 to 1023, as said below
- loc_bin: int32 [2048], P('tile'), may hold values from 0 to 4
Outputs:
- analysis: bfloat16 [1024, 256, 512], P('tile', 'mem')
Inputs may be any that keep to these rules, and one draw needn't show every extreme that they name: Block o lies in a tile of its own index of tile: obs_tile[o] // 4 == o // 8. `pair_tiles`: slot k's first tile i has i // 4 == k // 8; its second tile j differs from i and j // 4 - i // 4 lies in 0 to 2, equal to 2 for some slot. Pairs may repeat. `loc_bin`: bin 4 marks an empty slot.
All inputs are finite; a program needn't handle non-finite values.
Results may differ from a plain program's by a relative error of at most 0.0051.
Values may be sent and summed in bfloat16 or wider, within the bound.
A program may use at most 128 MiB of HBM per device.

v0:
```python
import jax
import jax.numpy as jnp
from jax import lax
from jax.sharding import PartitionSpec as P

MEMBERS = 256
HOPS = 2
NBIN = 4
RADIUS = 4


def from_behind(shard, axis, by):
    size = lax.axis_size(axis)
    pairs = [(i, i + by) for i in range(size) if 0 <= i + by < size]
    return lax.ppermute(shard, axis, pairs)


def weights_for(bins, points):
    positions = jnp.arange(points, dtype=jnp.int32)
    column = (positions % 32).astype(jnp.float32)
    levels = (positions // 32).astype(jnp.float32)
    along = (
        0.5 * RADIUS * bins.astype(jnp.float32)[:, None, None]
        + column[None, None, :]
        - column[None, :, None]
    )
    across = levels[None, None, :] - levels[None, :, None]
    weight = jnp.exp(-(along * along + across * across) / (2.0 * RADIUS * RADIUS))
    return jnp.where(bins[:, None, None] < NBIN, weight, 0.0)


def per_device(anomalies, innovations, obs_tile, pair_tiles, loc_bin):
    tile_count = anomalies.shape[0]
    points = anomalies.shape[2]
    tile_base = lax.axis_index("tile") * tile_count
    local_ids = jnp.arange(tile_count, dtype=jnp.int32)
    obs_onehot = (obs_tile[:, None] - tile_base == local_ids[None, :]).astype(jnp.bfloat16)
    forcing = jnp.einsum(
        "ot,omp->tmp", obs_onehot, innovations, preferred_element_type=jnp.float32
    ).astype(jnp.bfloat16)
    window_a = [anomalies]
    window_g = [forcing]
    for distance in range(1, HOPS + 1):
        fetched_a, fetched_g = from_behind((anomalies, forcing), "tile", -distance)
        window_a.append(fetched_a)
        window_g.append(fetched_g)
    window_a = jnp.concatenate(window_a, axis=0)
    window_g = jnp.concatenate(window_g, axis=0)
    first_local = pair_tiles[:, 0] - tile_base
    second_local = pair_tiles[:, 1] - tile_base
    whole_window = lax.all_gather(window_a, "mem", axis=1, tiled=True)
    first_a = jnp.take(whole_window, first_local, axis=0)
    second_a = jnp.take(whole_window, second_local, axis=0)
    cross = jnp.einsum("kmp,kmq->kpq", first_a, second_a, preferred_element_type=jnp.float32)
    own_whole = whole_window[:tile_count]
    self_cross = jnp.einsum(
        "tmp,tmq->tpq", own_whole, own_whole, preferred_element_type=jnp.float32
    )
    covar = (weights_for(loc_bin, points) * cross / (MEMBERS - 1)).astype(jnp.bfloat16)
    zero_bins = jnp.zeros((tile_count,), jnp.int32)
    own_covar = (weights_for(zero_bins, points) * self_cross / (MEMBERS - 1)).astype(jnp.bfloat16)
    first_g = jnp.take(forcing, first_local, axis=0)
    second_g = jnp.take(window_g, second_local, axis=0)
    to_first = jnp.einsum("kmq,kpq->kmp", second_g, covar, preferred_element_type=jnp.float32)
    to_second = jnp.einsum("kmp,kpq->kmq", first_g, covar, preferred_element_type=jnp.float32)
    first_onehot = (first_local[:, None] == local_ids[None, :]).astype(jnp.float32)
    window_ids = jnp.arange(window_a.shape[0], dtype=jnp.int32)
    second_onehot = (second_local[:, None] == window_ids[None, :]).astype(jnp.float32)
    own_total = jnp.einsum("tmq,tpq->tmp", forcing, own_covar, preferred_element_type=jnp.float32)
    own_total = own_total + jnp.einsum(
        "kt,kmp->tmp", first_onehot, to_first, precision=lax.Precision.HIGHEST
    )
    window_total = jnp.einsum(
        "kw,kmp->wmp", second_onehot, to_second, precision=lax.Precision.HIGHEST
    )
    own_total = own_total + window_total[:tile_count]
    for distance in range(1, HOPS + 1):
        block = window_total[distance * tile_count : (distance + 1) * tile_count]
        own_total = own_total + from_behind(block, "tile", distance)
    return (anomalies.astype(jnp.float32) + own_total).astype(jnp.bfloat16)


def solution(mesh):
    return jax.shard_map(
        per_device,
        mesh=mesh,
        in_specs=(
            P("tile", "mem", None),
            P("tile", "mem", None),
            P("tile"),
            P("tile", None),
            P("tile"),
        ),
        out_specs=P("tile", "mem", None),
        check_vma=False,
    )
```

profile of v0, /device:TPU:448, one launch (start us, length us, event | category | flops | bytes accessed | tf_op | source)
XLA Modules:
  0.0 161.1 jit_solution(11825369523886181278)
XLA Ops:
  6.5 7.7 %collective-permute-start = (bf16[4,128,512]{2,1,0:T(8,128)(2,1)}, bf16[4,128,512]{2,1,0:T(8,128)(2,1)S(1)}, u32[]{:S(2)}, u32[]{:S(2)}) collective-permute-start(bf16[4,128,512]{2,1,0:T(8,128)(2,1)} %param.7), channel_id=1, source_target_pairs={{1,0},{2,1},{3,2},{4,3},{5,4},{6,5},{7,6},{8,7},{9,8},{10,9},{11,1... | collective-permute-start | bytes 1572872 | tf_op jit(solution)/shard_map/ppermute | solution.py:15
  14.2 2.7 %collective-permute-start.1 = (bf16[4,128,512]{2,1,0:T(8,128)(2,1)}, bf16[4,128,512]{2,1,0:T(8,128)(2,1)S(1)}, u32[]{:S(2)}, u32[]{:S(2)}) collective-permute-start(bf16[4,128,512]{2,1,0:T(8,128)(2,1)} %param.7), channel_id=1, source_target_pairs={{2,0},{3,1},{4,2},{5,3},{6,4},{7,5},{8,6},{9,7},{10,8},{11,9},{12,... | collective-permute-start | bytes 1572872 | tf_op jit(solution)/shard_map/ppermute | solution.py:15
  17.6 15.9 %collective-permute-done = bf16[4,128,512]{2,1,0:T(8,128)(2,1)S(1)} collective-permute-done((bf16[4,128,512]{2,1,0:T(8,128)(2,1)}, bf16[4,128,512]{2,1,0:T(8,128)(2,1)S(1)}, u32[]{:S(2)}, u32[]{:S(2)}) %collective-permute-start) | collective-permute-done | bytes 524320 | tf_op jit(solution)/shard_map/ppermute | solution.py:15
  33.5 10.4 %collective-permute-done.1 = bf16[4,128,512]{2,1,0:T(8,128)(2,1)S(1)} collective-permute-done((bf16[4,128,512]{2,1,0:T(8,128)(2,1)}, bf16[4,128,512]{2,1,0:T(8,128)(2,1)S(1)}, u32[]{:S(2)}, u32[]{:S(2)}) %collective-permute-start.1) | collective-permute-done | bytes 524320 | tf_op jit(solution)/shard_map/ppermute | solution.py:15
  43.9 2.4 %pad_maximum_fusion.1 = bf16[12,128,512]{2,1,0:T(8,128)(2,1)} fusion(bf16[4,128,512]{2,1,0:T(8,128)(2,1)S(1)} %collective-permute-done.1, bf16[4,128,512]{2,1,0:T(8,128)(2,1)S(1)} %collective-permute-done, bf16[4,128,512]{2,1,0:T(8,128)(2,1)} %param.7), kind=kLoop, calls=%fused_computation.15 | loop fusion | flops 1572864 | bytes 3145728 | tf_op jit(solution)/shard_map/concatenate | solution.py:47
  47.1 8.9 %collective-permute-start.3 = (bf16[4,128,512]{2,0,1:T(4,128)(2,1)S(1)}, bf16[4,128,512]{2,0,1:T(4,128)(2,1)S(1)}, u32[]{:S(2)}, u32[]{:S(2)}) collective-permute-start(bf16[4,128,512]{2,0,1:T(4,128)(2,1)S(1)} %convolution_convert_fusion), channel_id=1, source_target_pairs={{2,0},{3,1},{4,2},{5,3},{6,4},{7,5},{8,6},{9,7},{10,8},{11,9},{12,... | collective-permute-start | bytes 1572872 | tf_op jit(solution)/shard_map/ppermute | solution.py:15
  55.9 1.9 %collective-permute-start.2 = (bf16[4,128,512]{2,0,1:T(4,128)(2,1)S(1)}, bf16[4,128,512]{2,0,1:T(4,128)(2,1)S(1)}, u32[]{:S(2)}, u32[]{:S(2)}) collective-permute-start(bf16[4,128,512]{2,0,1:T(4,128)(2,1)S(1)} %convolution_convert_fusion), channel_id=1, source_target_pairs={{1,0},{2,1},{3,2},{4,3},{5,4},{6,5},{7,6},{8,7},{9,8},{10,9},{11,1... | collective-permute-start | bytes 1572872 | tf_op jit(solution)/shard_map/ppermute | solution.py:15
  58.1 1.7 %gather_fusion.1 = bf16[8,128,512]{2,1,0:T(8,128)(2,1)} fusion(bf16[4,128,512]{2,1,0:T(8,128)(2,1)S(1)} %copy.14, s32[1024]{0:T(1024)S(1)} %pad_clamp_fusion), kind=kCustom, calls=%fused_computation.3 | custom fusion | bytes 2097184 | tf_op jit(solution)/shard_map/jit(_take)/gather | solution.py:62
  59.9 1.1 subtract_multiply_fusion
  61.0 7.3 %collective-permute-done.3 = bf16[4,128,512]{2,0,1:T(4,128)(2,1)S(1)} collective-permute-done((bf16[4,128,512]{2,0,1:T(4,128)(2,1)S(1)}, bf16[4,128,512]{2,0,1:T(4,128)(2,1)S(1)}, u32[]{:S(2)}, u32[]{:S(2)}) %collective-permute-start.3) | collective-permute-done | bytes 524320 | tf_op jit(solution)/shard_map/ppermute | solution.py:15
  68.3 9.1 %collective-permute-done.2 = bf16[4,128,512]{2,0,1:T(4,128)(2,1)S(1)} collective-permute-done((bf16[4,128,512]{2,0,1:T(4,128)(2,1)S(1)}, bf16[4,128,512]{2,0,1:T(4,128)(2,1)S(1)}, u32[]{:S(2)}, u32[]{:S(2)}) %collective-permute-start.2) | collective-permute-done | bytes 524320 | tf_op jit(solution)/shard_map/ppermute | solution.py:15
  79.3 1.7 %gather_fusion = bf16[8,128,512]{2,1,0:T(8,128)(2,1)} fusion(bf16[12,128,512]{2,1,0:T(8,128)(2,1)S(1)} %copy.15, s32[1024]{0:T(1024)S(1)} %pad_clamp_fusion.3), kind=kCustom, calls=%fused_computation.2 | custom fusion | bytes 2097184 | tf_op jit(solution)/shard_map/jit(_take)/gather | solution.py:63
  81.0 3.9 %gather_fusion.3 = bf16[8,256,512]{2,1,0:T(8,128)(2,1)} fusion(bf16[12,256,512]{2,1,0:T(8,128)(2,1)} %all-gather.2.cloned.1.call-done, s32[1024]{0:T(1024)S(1)} %pad_clamp_fusion.1), kind=kCustom, calls=%fused_computation.1.clone | custom fusion | bytes 4194336 | tf_op jit(solution)/shard_map/jit(_take)/gather | solution.py:53
  85.0 4.0 %gather_fusion.2 = bf16[8,256,512]{2,1,0:T(8,128)(2,1)} fusion(bf16[12,256,512]{2,1,0:T(8,128)(2,1)} %all-gather.2.cloned.1.call-done, s32[1024]{0:T(1024)S(1)} %pad_clamp_fusion.2), kind=kCustom, calls=%fused_computation.clone | custom fusion | bytes 4194336 | tf_op jit(solution)/shard_map/jit(_take)/gather | solution.py:52
  89.0 5.9 %multiply_convert_fusion = bf16[8,512,512]{2,1,0:T(8,128)(2,1)S(1)} fusion(f32[512,512]{1,0:T(8,128)S(1)} %copy-done.5, f32[512]{0:T(512)S(1)} %fusion.26, f32[8,512]{1,0:T(8,128)S(1)} %broadcast_add_fusion, pred[8]{0:T(512)(128)(4,1)S(1)} %broadcast_compare_fusion, bf16[8,256,512]{2,1,0:T(8,128)(2,1)} %gather_fusion.3, ...), kind=kOutput, calls=%fused_computation.4 | convolution fusion | flops 1094713344 | bytes 9455640 | tf_op jit(solution)/shard_map/kmp,kmq->kpq/dot_general | solution.py:54
  95.6 2.8 %fusion = f32[12,128,512]{2,0,1:T(8,128)S(1)} fusion(f32[8,128,512]{2,1,0:T(8,128)S(1)} %fusion.16, s32[8]{0:T(128)S(1)} %bitcast.29), kind=kOutput, calls=%fused_computation.7 | convolution fusion | flops 75497568 | bytes 5242912 | tf_op jit(solution)/shard_map/kw,kmp->wmp/dot_general | solution.py:73
  99.7 1.9 %collective-permute-start.5 = (f32[4,128,512]{2,1,0:T(8,128)S(1)}, f32[4,128,512]{2,1,0:T(8,128)S(1)}, u32[]{:S(2)}, u32[]{:S(2)}) collective-permute-start(f32[4,128,512]{2,1,0:T(8,128)S(1)} %copy.27), channel_id=1, source_target_pairs={{0,2},{1,3},{2,4},{3,5},{4,6},{5,7},{6,8},{7,9},{8,10},{9,11},{10,... | collective-permute-start | bytes 3145736 | tf_op jit(solution)/shard_map/ppermute | solution.py:15
  101.6 3.4 %collective-permute-start.4 = (f32[4,128,512]{2,1,0:T(8,128)S(1)}, f32[4,128,512]{2,1,0:T(8,128)S(1)}, u32[]{:S(2)}, u32[]{:S(2)}) collective-permute-start(f32[4,128,512]{2,1,0:T(8,128)S(1)} %copy.26), channel_id=1, source_target_pairs={{0,1},{1,2},{2,3},{3,4},{4,5},{5,6},{6,7},{7,8},{8,9},{9,10},{10,1... | collective-permute-start | bytes 3145736 | tf_op jit(solution)/shard_map/ppermute | solution.py:15
  105.1 1.5 fusion.18
  106.6 2.2 %fusion.2 = f32[4,128,512]{2,0,1:T(4,128)S(1)} fusion(f32[8,128,512]{2,1,0:T(8,128)S(1)} %fusion.18, s32[8]{0:T(128)S(1)} %bitcast.30), kind=kOutput, calls=%fused_computation.9 | convolution fusion | flops 25165856 | bytes 3145760 | tf_op jit(solution)/shard_map/kt,kmp->tmp/dot_general | solution.py:70
  108.8 1.2 multiply_convert_fusion.1
  110.1 20.6 %collective-permute-done.5 = f32[4,128,512]{2,1,0:T(8,128)S(1)} collective-permute-done((f32[4,128,512]{2,1,0:T(8,128)S(1)}, f32[4,128,512]{2,1,0:T(8,128)S(1)}, u32[]{:S(2)}, u32[]{:S(2)}) %collective-permute-start.5) | collective-permute-done | bytes 1048608 | tf_op jit(solution)/shard_map/ppermute | solution.py:15
  130.6 21.5 %collective-permute-done.4 = f32[4,128,512]{2,1,0:T(8,128)S(1)} collective-permute-done((f32[4,128,512]{2,1,0:T(8,128)S(1)}, f32[4,128,512]{2,1,0:T(8,128)S(1)}, u32[]{:S(2)}, u32[]{:S(2)}) %collective-permute-start.4) | collective-permute-done | bytes 1048608 | tf_op jit(solution)/shard_map/ppermute | solution.py:15
  152.1 2.1 %fusion.12 = bf16[4,128,512]{2,1,0:T(8,128)(2,1)} fusion(f32[4,128,512]{2,1,0:T(8,128)S(1)} %collective-permute-done.5, f32[4,128,512]{2,1,0:T(8,128)S(1)} %collective-permute-done.4, bf16[4,512,512]{2,1,0:T(8,128)(2,1)S(1)} %multiply_convert_fusion.1, f32[4,128,512]{2,0,1:T(4,128)S(1)} %get-tuple-element.10, f32[4,128,512]{2,0,1:T(4,128)S(1)} %fusion.2, ...), kind=kOutput, calls=%fused_computation.21 | convolution fusion | flops 270270464 | bytes 7864320 | tf_op jit(solution)/shard_map/tmq,tpq->tmp/dot_general | solution.py:69
  (42 shorter events, 5.6 us)
Async XLA Ops:
  6.5 39.8 %copy-start = (bf16[8,128,512]{2,1,0:T(8,128)(2,1)S(1)}, bf16[8,128,512]{2,1,0:T(8,128)(2,1)}, u32[]{:S(2)}) copy-start(bf16[8,128,512]{2,1,0:T(8,128)(2,1)} %param.8) | copy-start | bytes 3145732
  6.5 74.5 %all-gather.2.cloned.1.call-start = ((), (), s32[]{:S(2)}) async-start(), calls=%async_computation | async-start | bytes 4718592 | tf_op jit(solution)/shard_map/all_gather | solution.py:51
  6.5 27.0 %collective-permute-start = (bf16[4,128,512]{2,1,0:T(8,128)(2,1)}, bf16[4,128,512]{2,1,0:T(8,128)(2,1)S(1)}, u32[]{:S(2)}, u32[]{:S(2)}) collective-permute-start(bf16[4,128,512]{2,1,0:T(8,128)(2,1)} %param.7), channel_id=1, source_target_pairs={{1,0},{2,1},{3,2},{4,3},{5,4},{6,5},{7,6},{8,7},{9,8},{10,9},{11,1... | collective-permute-start | bytes 1572872 | tf_op jit(solution)/shard_map/ppermute | solution.py:15
  14.2 29.7 %collective-permute-start.1 = (bf16[4,128,512]{2,1,0:T(8,128)(2,1)}, bf16[4,128,512]{2,1,0:T(8,128)(2,1)S(1)}, u32[]{:S(2)}, u32[]{:S(2)}) collective-permute-start(bf16[4,128,512]{2,1,0:T(8,128)(2,1)} %param.7), channel_id=1, source_target_pairs={{2,0},{3,1},{4,2},{5,3},{6,4},{7,5},{8,6},{9,7},{10,8},{11,9},{12,... | collective-permute-start | bytes 1572872 | tf_op jit(solution)/shard_map/ppermute | solution.py:15
  17.6 40.2 %copy-start.6 = (s32[8,2]{0,1:T(2,128)S(1)}, s32[8,2]{0,1:T(2,128)}, u32[]{:S(2)}) copy-start(s32[8,2]{0,1:T(2,128)} %param.10) | copy-start | bytes 196
  17.6 40.4 %copy-start.7 = (s32[8]{0:T(128)S(1)}, s32[8]{0:T(128)}, u32[]{:S(2)}) copy-start(s32[8]{0:T(128)} %param.11) | copy-start | bytes 100
  47.1 21.2 %collective-permute-start.3 = (bf16[4,128,512]{2,0,1:T(4,128)(2,1)S(1)}, bf16[4,128,512]{2,0,1:T(4,128)(2,1)S(1)}, u32[]{:S(2)}, u32[]{:S(2)}) collective-permute-start(bf16[4,128,512]{2,0,1:T(4,128)(2,1)S(1)} %convolution_convert_fusion), channel_id=1, source_target_pairs={{2,0},{3,1},{4,2},{5,3},{6,4},{7,5},{8,6},{9,7},{10,8},{11,9},{12,... | collective-permute-start | bytes 1572872 | tf_op jit(solution)/shard_map/ppermute | solution.py:15
  55.9 21.5 %collective-permute-start.2 = (bf16[4,128,512]{2,0,1:T(4,128)(2,1)S(1)}, bf16[4,128,512]{2,0,1:T(4,128)(2,1)S(1)}, u32[]{:S(2)}, u32[]{:S(2)}) collective-permute-start(bf16[4,128,512]{2,0,1:T(4,128)(2,1)S(1)} %convolution_convert_fusion), channel_id=1, source_target_pairs={{1,0},{2,1},{3,2},{4,3},{5,4},{6,5},{7,6},{8,7},{9,8},{10,9},{11,1... | collective-permute-start | bytes 1572872 | tf_op jit(solution)/shard_map/ppermute | solution.py:15
  85.0 4.0 %copy-start.5 = (f32[512,512]{1,0:T(8,128)S(1)}, f32[512,512]{1,0:T(8,128)}, u32[]{:S(2)}) copy-start(f32[512,512]{1,0:T(8,128)} %subtract_multiply_fusion) | copy-start | bytes 3145732
  89.0 5.9 %copy-start.3 = (bf16[8,128,512]{2,1,0:T(8,128)(2,1)S(1)}, bf16[8,128,512]{2,1,0:T(8,128)(2,1)}, u32[]{:S(2)}) copy-start(bf16[8,128,512]{2,1,0:T(8,128)(2,1)} %gather_fusion.1) | copy-start | bytes 3145732
  99.0 6.1 %copy-start.2 = (bf16[8,128,512]{2,1,0:T(8,128)(2,1)S(1)}, bf16[8,128,512]{2,1,0:T(8,128)(2,1)}, u32[]{:S(2)}) copy-start(bf16[8,128,512]{2,1,0:T(8,128)(2,1)} %gather_fusion) | copy-start | bytes 3145732
  99.7 30.9 %collective-permute-start.5 = (f32[4,128,512]{2,1,0:T(8,128)S(1)}, f32[4,128,512]{2,1,0:T(8,128)S(1)}, u32[]{:S(2)}, u32[]{:S(2)}) collective-permute-start(f32[4,128,512]{2,1,0:T(8,128)S(1)} %copy.27), channel_id=1, source_target_pairs={{0,2},{1,3},{2,4},{3,5},{4,6},{5,7},{6,8},{7,9},{8,10},{9,11},{10,... | collective-permute-start | bytes 3145736 | tf_op jit(solution)/shard_map/ppermute | solution.py:15
  101.6 50.5 %collective-permute-start.4 = (f32[4,128,512]{2,1,0:T(8,128)S(1)}, f32[4,128,512]{2,1,0:T(8,128)S(1)}, u32[]{:S(2)}, u32[]{:S(2)}) collective-permute-start(f32[4,128,512]{2,1,0:T(8,128)S(1)} %copy.26), channel_id=1, source_target_pairs={{0,1},{1,2},{2,3},{3,4},{4,5},{5,6},{6,7},{7,8},{8,9},{9,10},{10,1... | collective-permute-start | bytes 3145736 | tf_op jit(solution)/shard_map/ppermute | solution.py:15
  106.6 2.2 %copy-start.1 = (bf16[12,256,512]{2,1,0:T(8,128)(2,1)S(1)}, bf16[12,256,512]{2,1,0:T(8,128)(2,1)}, u32[]{:S(2)}) copy-start(bf16[12,256,512]{2,1,0:T(8,128)(2,1)} %all-gather.2.cloned.1.call-done) | copy-start | bytes 9437188
  108.8 43.3 %copy-start.4 = (bf16[4,128,512]{2,1,0:T(8,128)(2,1)S(1)}, bf16[4,128,512]{2,1,0:T(8,128)(2,1)}, u32[]{:S(2)}) copy-start(bf16[4,128,512]{2,1,0:T(8,128)(2,1)} %param.7) | copy-start | bytes 1572868
Sparse Core Ops, SparseCore 0:
  46.4 19.5 all-gather.1
where the time goes:
time: 161 us
  waiting for transfers between devices  84.8 us (53%)
  starting transfers between devices  26.5 us (16%)
  matrix products  17.2 us (11%)
  between operations  13.7 us (9%)
  local copies, waits for them, and re-layouts  13.5 us (8%)
  other arithmetic  5.41 us (3%)
    ppermute x6, waiting for transfers between devices, from_behind(): return lax.ppermute(shard, axis, pairs)  84.7 us
    ppermute x6, starting transfers between devices, from_behind(): return lax.ppermute(shard, axis, pairs)  26.5 us
    dot_general x1, matrix products, per_device(): jnp.einsum('kmp,kmq->kpq', first_a, second_a, preferred_element_type=jnp....  5.86 us
    gather x1, local copies, waits for them, and re-layouts, per_device(): first_a = jnp.take(whole_window, first_local, axis=0)  4 us
    gather x1, local copies, waits for them, and re-layouts, per_device(): second_a = jnp.take(whole_window, second_local, axis=0)  3.92 us
  transfers between devices with their start and end apart: 7, of which 6 were waited for; matrix products, arithmetic and copies ran while one was open for 8% of the time, Pallas kernels for 0%

commit v1 on v0

v1 whole, which is shorter than its diff:
```python
import functools

import jax
import jax.numpy as jnp
from jax import lax
from jax.experimental import pallas as pl
from jax.experimental.pallas import tpu as pltpu
from jax.sharding import PartitionSpec as P

MEMBERS = 256
POINTS = 512
NBIN = 4
RADIUS = 4
TILES = 4
SLOTS = 8
BLOCKS = 8
HALF = MEMBERS // 2
CHUNKS = 2
ROWS = HALF // CHUNKS
BAND = 128
MESH = pl.DeviceIdType.MESH


def kernel(
    obs_ref, pair_ref, bin_ref, a_ref, innov_ref, out_ref,
    before_pair, before_bin, a_win, a_turned, g_win0, g_win1, rho, cov, own_cov, to_first, to_second,
    i_left, i_right, from_left, from_right, own_total,
    a_send, a_recv, relay_send, relay_recv, g_send, g_recv, i_send, i_recv, info_send, info_recv,
):
    core = lax.axis_index("mem")
    me = lax.axis_index("tile")
    size = lax.axis_size("tile")
    right = (core, lax.rem(me + 1, size))
    left = (core, lax.rem(me + size - 1, size))
    sibling = (1 - core, me)
    g_win = (g_win0, g_win1)

    def send(src, dst, send_sem, recv_sem, device):
        return pltpu.make_async_remote_copy(
            src_ref=src, dst_ref=dst, send_sem=send_sem, recv_sem=recv_sem, device_id=device, device_id_type=MESH
        )

    barrier = pltpu.get_barrier_semaphore()
    for device in (left, right, sibling):
        pl.semaphore_signal(barrier, inc=1, device_id=device, device_id_type=MESH)
    pl.semaphore_wait(barrier, 3)

    mine = pl.ds(pl.multiple_of(core * HALF, HALF), HALF)
    a_out = []
    for t in range(TILES):
        for side, (device, slot) in enumerate(((right, t), (left, 2 * TILES + t), (sibling, TILES + t))):
            a_out.append(send(a_ref.at[t], a_win.at[slot, mine], a_send.at[side, t], a_recv.at[side, t], device))
            a_out[-1].start()
    info_out = [
        send(pair_ref, before_pair, info_send.at[0], info_recv.at[0], right),
        send(bin_ref, before_bin, info_send.at[1], info_recv.at[1], right),
    ]
    for copy in info_out:
        copy.start()

    base = me * TILES
    g_out = []
    for h in range(CHUNKS):
        for t in range(TILES):
            total = jnp.zeros((ROWS, POINTS), jnp.float32)
            for o in range(BLOCKS):
                share = jnp.where(obs_ref[o] - base == t, 1.0, 0.0).astype(jnp.float32)
                total = total + share * innov_ref[o, h * ROWS : (h + 1) * ROWS, :].astype(jnp.float32)
            g_win[h][TILES + t] = total.astype(jnp.bfloat16)
        here = g_win[h].at[TILES : 2 * TILES]
        for side, (device, slot) in enumerate(((right, 0), (left, 2 * TILES))):
            g_out.append(send(here, g_win[h].at[slot : slot + TILES], g_send.at[side, h], g_recv.at[side, h], device))
            g_out[-1].start()

    for t in range(TILES):
        a_win[TILES + t, mine] = a_ref[t]

    def weigh(n, _):
        b = n // (POINTS // BAND)
        start = pl.multiple_of(lax.rem(n, POINTS // BAND) * BAND, BAND)
        p = lax.broadcasted_iota(jnp.int32, (BAND, POINTS), 0) + start
        q = lax.broadcasted_iota(jnp.int32, (BAND, POINTS), 1)
        along = ((q & 31) - (p & 31)).astype(jnp.float32) + 0.5 * RADIUS * b.astype(jnp.float32)
        across = ((q >> 5) - (p >> 5)).astype(jnp.float32)
        weight = jnp.exp(-(along * along + across * across) / (2.0 * RADIUS * RADIUS))
        rho[b, pl.ds(start, BAND), :] = weight * (1.0 / (MEMBERS - 1))
        return 0

    lax.fori_loop(0, NBIN * (POINTS // BAND), weigh, 0)

    def product(turned, second, weights_of, target):
        for band in range(POINTS // BAND):
            rows = slice(band * BAND, (band + 1) * BAND)
            cross = jnp.dot(turned(rows), second, preferred_element_type=jnp.float32)
            target[rows, :] = (weights_of(rows) * cross).astype(jnp.bfloat16)

    for t in range(TILES):
        a_out[3 * t + 2].wait_recv()

    def own_product(t, _):
        tile = a_win[TILES + t]
        a_turned[TILES + t] = tile.T
        product(lambda rows: a_turned[TILES + t, rows, :], tile, lambda rows: rho[0, rows, :], own_cov.at[t])
        return 0

    lax.fori_loop(0, TILES, own_product, 0)

    relays = []
    for t in range(TILES):
        for side, slot in ((0, t), (1, 2 * TILES + t)):
            a_out[3 * t + side].wait_recv()
            here = a_win.at[slot, mine]
            relays.append(send(here, here, relay_send.at[side, t], relay_recv.at[side, t], sibling))
            relays[-1].start()
    for copy in info_out:
        copy.wait_recv()
    for copy in relays:
        copy.wait_recv()

    def turn(t, _):
        a_turned[t] = a_win[t].T
        return 0

    lax.fori_loop(0, TILES, turn, 0)

    base_before = lax.rem(me + size - 1, size) * TILES
    shift = base - TILES

    def slot_of(n):
        own = (pair_ref[n, 0] - shift, pair_ref[n, 1] - shift, bin_ref[n])
        far = (before_pair[n, 0] - base_before, before_pair[n, 1] - base_before, before_bin[n])
        return own, far

    def inside(first, second, b):
        return jnp.clip(first, 0, 2 * TILES - 1), jnp.clip(second, 0, 3 * TILES - 1), jnp.clip(b, 0, NBIN - 1)

    def covariance(n, _):
        for k, ends in enumerate(slot_of(n)):
            first, second, b = inside(*ends)
            product(
                lambda rows: a_turned[first, rows, :], a_win[second], lambda rows: rho[b, rows, :], cov.at[k * SLOTS + n]
            )
        return 0

    lax.fori_loop(0, SLOTS, covariance, 0)

    i_out = []
    nn = (((1,), (0,)), ((), ()))
    nt = (((1,), (1,)), ((), ()))
    for h in range(CHUNKS):
        g_out[2 * h].wait_recv()
        g_out[2 * h + 1].wait_recv()

        def increments(n, _):
            for k, ends in enumerate(slot_of(n)):
                first, second, _ = inside(*ends)
                matrix = cov[k * SLOTS + n]
                to_first[k * SLOTS + n] = lax.dot_general(
                    g_win[h][second], matrix, nt, preferred_element_type=jnp.float32
                )
                to_second[k * SLOTS + n] = lax.dot_general(
                    g_win[h][first], matrix, nn, preferred_element_type=jnp.float32
                )
            return 0

        lax.fori_loop(0, SLOTS, increments, 0)

        slots = [slot_of(n) for n in range(SLOTS)]

        def hit(end, tile, bin_, alive):
            return jnp.where((end == tile) & (bin_ < NBIN) & alive, 1.0, 0.0).astype(jnp.float32)

        near = [pair_ref[n, 1] - base < 2 * TILES for n in range(SLOTS)]
        away = [before_pair[n, 1] - base_before >= 2 * TILES for n in range(SLOTS)]
        for t in range(TILES):
            total = jnp.zeros((ROWS, POINTS), jnp.float32)
            for n, (_, (first, _, b)) in enumerate(slots):
                total = total + hit(first, t, b, away[n]) * to_first[SLOTS + n]
            i_left[h, t] = total.astype(jnp.bfloat16)
            total = jnp.zeros((ROWS, POINTS), jnp.float32)
            for n, ((_, second, b), (_, far_second, far_b)) in enumerate(slots):
                total = total + hit(second, 2 * TILES + t, b, near[n]) * to_second[n]
                total = total + hit(far_second, 2 * TILES + t, far_b, away[n]) * to_second[SLOTS + n]
            i_right[h, t] = total.astype(jnp.bfloat16)
        for side, (device, src, dst) in enumerate(((right, i_right, from_left), (left, i_left, from_right))):
            i_out.append(send(src.at[h], dst.at[h], i_send.at[side, h], i_recv.at[side, h], device))
            i_out[-1].start()
        for t in range(TILES):
            rows = slice(h * ROWS, (h + 1) * ROWS)
            total = jnp.dot(g_win[h][TILES + t], own_cov[t], preferred_element_type=jnp.float32)
            total = total + a_ref[t, rows, :].astype(jnp.float32)
            for n, ((first, second, b), _) in enumerate(slots):
                total = total + hit(first, TILES + t, b, near[n]) * to_first[n]
                total = total + hit(second, TILES + t, b, near[n]) * to_second[n]
            own_total[h, t] = total

    for h in range(CHUNKS):
        i_out[2 * h].wait_recv()
        i_out[2 * h + 1].wait_recv()
        for t in range(TILES):
            total = own_total[h, t] + from_left[h, t].astype(jnp.float32) + from_right[h, t].astype(jnp.float32)
            out_ref[t, h * ROWS : (h + 1) * ROWS, :] = total.astype(jnp.bfloat16)
    for copy in a_out + info_out + g_out + relays + i_out:
        copy.wait_send()


def per_device(anomalies, innovations, obs_tile, pair_tiles, loc_bin):
    bf16, f32 = jnp.bfloat16, jnp.float32
    vmem, smem = pl.BlockSpec(memory_space=pltpu.VMEM), pl.BlockSpec(memory_space=pltpu.SMEM)
    dma = pltpu.SemaphoreType.DMA
    return pl.pallas_call(
        kernel,
        name="analysis",
        out_shape=jax.ShapeDtypeStruct(anomalies.shape, bf16),
        in_specs=[smem, smem, smem, vmem, vmem],
        out_specs=vmem,
        scratch_shapes=[
            pltpu.SMEM((SLOTS, 2), jnp.int32),
            pltpu.SMEM((SLOTS,), jnp.int32),
            pltpu.VMEM((3 * TILES, MEMBERS, POINTS), bf16),
            pltpu.VMEM((2 * TILES, POINTS, MEMBERS), bf16),
            pltpu.VMEM((3 * TILES, ROWS, POINTS), bf16),
            pltpu.VMEM((3 * TILES, ROWS, POINTS), bf16),
            pltpu.VMEM((NBIN, POINTS, POINTS), f32),
            pltpu.VMEM((2 * SLOTS, POINTS, POINTS), bf16),
            pltpu.VMEM((TILES, POINTS, POINTS), bf16),
            pltpu.VMEM((2 * SLOTS, ROWS, POINTS), f32),
            pltpu.VMEM((2 * SLOTS, ROWS, POINTS), f32),
            pltpu.VMEM((CHUNKS, TILES, ROWS, POINTS), bf16),
            pltpu.VMEM((CHUNKS, TILES, ROWS, POINTS), bf16),
            pltpu.VMEM((CHUNKS, TILES, ROWS, POINTS), bf16),
            pltpu.VMEM((CHUNKS, TILES, ROWS, POINTS), bf16),
            pltpu.VMEM((CHUNKS, TILES, ROWS, POINTS), f32),
            dma((3, TILES)), dma((3, TILES)),
            dma((2, TILES)), dma((2, TILES)),
            dma((2, CHUNKS)), dma((2, CHUNKS)),
            dma((2, CHUNKS)), dma((2, CHUNKS)),
            dma((2,)), dma((2,)),
        ],
        compiler_params=pltpu.CompilerParams(collective_id=0, has_side_effects=True, vmem_limit_bytes=56 << 20),
    )(obs_tile, pair_tiles, loc_bin, anomalies, innovations)


def solution(mesh):
    return jax.shard_map(
        per_device,
        mesh=mesh,
        in_specs=(
            P("tile", "mem", None),
            P("tile", "mem", None),
            P("tile"),
            P("tile", None),
            P("tile"),
        ),
        out_specs=P("tile", "mem", None),
        check_vma=False,
    )
```

time: 161 us -> 66.5 us (0.41)
  the two profiles are of different devices: /device:TPU:448 before, /device:TPU:1 now
where the time goes in v1:
time: 66.5 us; the launch traced here: 66.3 us
  Pallas kernels  63 us (95%)
  local copies, waits for them, and re-layouts  3.21 us (5%)
    pallas_call x1, Pallas kernels, per_device(): pl.pallas_call(kernel, name='analysis', out_shape=jax.ShapeDtypeStruct(an...  63 us
    unnamed x2, local copies, waits for them, and re-layouts  3.21 us

profile of v1, /device:TPU:1, one launch (start us, length us, event | category | flops | bytes accessed | tf_op | source)
XLA Modules:
  0.0 66.3 jit_solution(6333823003234842185)
XLA Ops:
  0.0 1.3 %copy.6.pair_ref = s32[8,2]{1,0:T(8,128)} copy(s32[8,2]{0,1:T(2,128)} %param.8) | data formatting | bytes 128 | tf_op args[3]
  1.3 63.0 %analysis.1 = bf16[4,128,512]{2,1,0:T(8,128)(2,1)} custom-call(s32[8]{0:T(128)} %obs_ref.1, s32[8,2]{1,0:T(8,128)} %copy.6.pair_ref, s32[8]{0:T(128)} %bin_ref.1, bf16[4,128,512]{2,1,0:T(8,128)(2,1)} %a_ref.1, bf16[8,128,512]{2,1,0:T(8,128)(2,1)} %innov_ref.1), custom_call_target="tpu_custom_call" | custom-call | tf_op jit(solution)/shard_map/analysis/pallas_call | solution.py:211
  64.4 1.9 %copy.8 = bf16[4,128,512]{2,1,0:T(8,128)(2,1)} copy(bf16[4,128,512]{2,1,0:T(8,128)(2,1)} %analysis.1) | data formatting | bytes 1048576

commit v2 on v1

--- a/solution.py
+++ b/solution.py
@@ -40,26 +40,65 @@
             src_ref=src, dst_ref=dst, send_sem=send_sem, recv_sem=recv_sem, device_id=device, device_id_type=MESH
         )
 
+    not_first, not_last = me > 0, me < size - 1
+    to_side, from_side = (not_last, not_first), (not_first, not_last)
+
     barrier = pltpu.get_barrier_semaphore()
-    for device in (left, right, sibling):
-        pl.semaphore_signal(barrier, inc=1, device_id=device, device_id_type=MESH)
-    pl.semaphore_wait(barrier, 3)
+    for device, there in ((left, not_first), (right, not_last), (sibling, None)):
+
+        def greet():
+            pl.semaphore_signal(barrier, inc=1, device_id=device, device_id_type=MESH)
+
+        greet() if there is None else pl.when(there)(greet)
+    both = not_first & not_last
+
+    @pl.when(both)
+    def _():
+        pl.semaphore_wait(barrier, 3)
+
+    @pl.when(jnp.logical_not(both))
+    def _():
+        pl.semaphore_wait(barrier, 2)
 
     mine = pl.ds(pl.multiple_of(core * HALF, HALF), HALF)
-    a_out = []
+    a_out = [[], [], []]
     for t in range(TILES):
         for side, (device, slot) in enumerate(((right, t), (left, 2 * TILES + t), (sibling, TILES + t))):
-            a_out.append(send(a_ref.at[t], a_win.at[slot, mine], a_send.at[side, t], a_recv.at[side, t], device))
-            a_out[-1].start()
+            a_out[side].append(send(a_ref.at[t], a_win.at[slot, mine], a_send.at[side, t], a_recv.at[side, t], device))
     info_out = [
         send(pair_ref, before_pair, info_send.at[0], info_recv.at[0], right),
         send(bin_ref, before_bin, info_send.at[1], info_recv.at[1], right),
     ]
-    for copy in info_out:
-        copy.start()
+    for t in range(TILES):
+        for side in range(2):
+            pl.when(to_side[side])(a_out[side][t].start)
+        a_out[2][t].start()
+
+    @pl.when(not_last)
+    def _():
+        for copy in info_out:
+            copy.start()
+
+    @pl.when(me == 0)
+    def _():
+        a_win[:TILES] = jnp.zeros((TILES, MEMBERS, POINTS), jnp.bfloat16)
+        for h in range(CHUNKS):
+            g_win[h][:TILES] = jnp.zeros((TILES, ROWS, POINTS), jnp.bfloat16)
+        from_left[...] = jnp.zeros_like(from_left)
+        for n in range(SLOTS):
+            before_bin[n] = NBIN
+            before_pair[n, 0] = 0
+            before_pair[n, 1] = 0
+
+    @pl.when(me == size - 1)
+    def _():
+        a_win[2 * TILES :] = jnp.zeros((TILES, MEMBERS, POINTS), jnp.bfloat16)
+        for h in range(CHUNKS):
+            g_win[h][2 * TILES :] = jnp.zeros((TILES, ROWS, POINTS), jnp.bfloat16)
+        from_right[...] = jnp.zeros_like(from_right)
 
     base = me * TILES
-    g_out = []
+    g_out = [[], []]
     for h in range(CHUNKS):
         for t in range(TILES):
             total = jnp.zeros((ROWS, POINTS), jnp.float32)
@@ -69,8 +108,9 @@
             g_win[h][TILES + t] = total.astype(jnp.bfloat16)
         here = g_win[h].at[TILES : 2 * TILES]
         for side, (device, slot) in enumerate(((right, 0), (left, 2 * TILES))):
-            g_out.append(send(here, g_win[h].at[slot : slot + TILES], g_send.at[side, h], g_recv.at[side, h], device))
-            g_out[-1].start()
+            there = g_win[h].at[slot : slot + TILES]
+            g_out[side].append(send(here, there, g_send.at[side, h], g_recv.at[side, h], device))
+            pl.when(to_side[side])(g_out[side][h].start)
 
     for t in range(TILES):
         a_win[TILES + t, mine] = a_ref[t]
@@ -95,7 +135,7 @@
             target[rows, :] = (weights_of(rows) * cross).astype(jnp.bfloat16)
 
     for t in range(TILES):
-        a_out[3 * t + 2].wait_recv()
+        a_out[2][t].wait_recv()
 
     def own_product(t, _):
         tile = a_win[TILES + t]
@@ -105,17 +145,26 @@
 
     lax.fori_loop(0, TILES, own_product, 0)
 
-    relays = []
+    relays = [[], []]
     for t in range(TILES):
         for side, slot in ((0, t), (1, 2 * TILES + t)):
-            a_out[3 * t + side].wait_recv()
             here = a_win.at[slot, mine]
-            relays.append(send(here, here, relay_send.at[side, t], relay_recv.at[side, t], sibling))
-            relays[-1].start()
-    for copy in info_out:
-        copy.wait_recv()
-    for copy in relays:
-        copy.wait_recv()
+            relays[side].append(send(here, here, relay_send.at[side, t], relay_recv.at[side, t], sibling))
+
+            @pl.when(from_side[side])
+            def _():
+                a_out[side][t].wait_recv()
+                relays[side][t].start()
+
+    @pl.when(not_first)
+    def _():
+        for copy in info_out + relays[0]:
+            copy.wait_recv()
+
+    @pl.when(not_last)
+    def _():
+        for copy in relays[1]:
+            copy.wait_recv()
 
     def turn(t, _):
         a_turned[t] = a_win[t].T
@@ -144,12 +193,12 @@
 
     lax.fori_loop(0, SLOTS, covariance, 0)
 
-    i_out = []
+    i_out = [[], []]
     nn = (((1,), (0,)), ((), ()))
     nt = (((1,), (1,)), ((), ()))
     for h in range(CHUNKS):
-        g_out[2 * h].wait_recv()
-        g_out[2 * h + 1].wait_recv()
+        for side in range(2):
+            pl.when(from_side[side])(g_out[side][h].wait_recv)
 
         def increments(n, _):
             for k, ends in enumerate(slot_of(n)):
@@ -183,8 +232,8 @@
                 total = total + hit(far_second, 2 * TILES + t, far_b, away[n]) * to_second[SLOTS + n]
             i_right[h, t] = total.astype(jnp.bfloat16)
         for side, (device, src, dst) in enumerate(((right, i_right, from_left), (left, i_left, from_right))):
-            i_out.append(send(src.at[h], dst.at[h], i_send.at[side, h], i_recv.at[side, h], device))
-            i_out[-1].start()
+            i_out[side].append(send(src.at[h], dst.at[h], i_send.at[side, h], i_recv.at[side, h], device))
+            pl.when(to_side[side])(i_out[side][h].start)
         for t in range(TILES):
             rows = slice(h * ROWS, (h + 1) * ROWS)
             total = jnp.dot(g_win[h][TILES + t], own_cov[t], preferred_element_type=jnp.float32)
@@ -195,13 +244,30 @@
             own_total[h, t] = total
 
     for h in range(CHUNKS):
-        i_out[2 * h].wait_recv()
-        i_out[2 * h + 1].wait_recv()
+        for side in range(2):
+            pl.when(from_side[side])(i_out[side][h].wait_recv)
         for t in range(TILES):
             total = own_total[h, t] + from_left[h, t].astype(jnp.float32) + from_right[h, t].astype(jnp.float32)
             out_ref[t, h * ROWS : (h + 1) * ROWS, :] = total.astype(jnp.bfloat16)
-    for copy in a_out + info_out + g_out + relays + i_out:
+
+    for copy in a_out[2]:
         copy.wait_send()
+    for side in range(2):
+
+        @pl.when(to_side[side])
+        def _():
+            for copy in a_out[side] + g_out[side] + i_out[side]:
+                copy.wait_send()
+
+        @pl.when(from_side[side])
+        def _():
+            for copy in relays[side]:
+                copy.wait_send()
+
+    @pl.when(not_last)
+    def _():
+        for copy in info_out:
+            copy.wait_send()
 
 
 def per_device(anomalies, innovations, obs_tile, pair_tiles, loc_bin):

time: 66.5 us -> 56.9 us (0.86)
  the two profiles are of different devices: /device:TPU:1 before, /device:TPU:448 now
where the time goes in v2:
time: 56.9 us; the launch traced here: 56.3 us
  Pallas kernels  53.1 us (93%)
  local copies, waits for them, and re-layouts  3.21 us (6%)
    pallas_call x1, Pallas kernels, per_device(): pl.pallas_call(kernel, name='analysis', out_shape=jax.ShapeDtypeStruct(an...  53.1 us
    unnamed x2, local copies, waits for them, and re-layouts  3.21 us

profile of v2, /device:TPU:448, one launch (start us, length us, event | category | flops | bytes accessed | tf_op | source)
XLA Modules:
  0.0 56.3 jit_solution(8064952803019873969)
XLA Ops:
  0.0 1.3 %copy.6.pair_ref = s32[8,2]{1,0:T(8,128)} copy(s32[8,2]{0,1:T(2,128)} %param.8) | data formatting | bytes 128 | tf_op args[3]
  1.3 53.1 %analysis.1 = bf16[4,128,512]{2,1,0:T(8,128)(2,1)} custom-call(s32[8]{0:T(128)} %obs_ref.1, s32[8,2]{1,0:T(8,128)} %copy.6.pair_ref, s32[8]{0:T(128)} %bin_ref.1, bf16[4,128,512]{2,1,0:T(8,128)(2,1)} %a_ref.1, bf16[8,128,512]{2,1,0:T(8,128)(2,1)} %innov_ref.1), custom_call_target="tpu_custom_call" | custom-call | tf_op jit(solution)/shard_map/analysis/pallas_call | solution.py:277
  54.5 1.9 %copy.8 = bf16[4,128,512]{2,1,0:T(8,128)(2,1)} copy(bf16[4,128,512]{2,1,0:T(8,128)(2,1)} %analysis.1) | data formatting | bytes 1048576

commit v3 on v2

--- a/solution.py
+++ b/solution.py
@@ -22,10 +22,10 @@
 
 
 def kernel(
-    obs_ref, pair_ref, bin_ref, a_ref, innov_ref, out_ref,
-    before_pair, before_bin, a_win, a_turned, g_win0, g_win1, rho, cov, own_cov, to_first, to_second,
+    obs_ref, pair_ref, bin_ref, a_ref, innov_hbm, out_ref,
+    innov_ref, before_pair, before_bin, a_win, a_turned, g_win0, g_win1, rho, cov, cov_turned, own_cov, to_first, to_second,
     i_left, i_right, from_left, from_right, own_total,
-    a_send, a_recv, relay_send, relay_recv, g_send, g_recv, i_send, i_recv, info_send, info_recv,
+    a_send, a_recv, relay_send, relay_recv, g_send, g_recv, i_send, i_recv, info_send, info_recv, load_sem,
 ):
     core = lax.axis_index("mem")
     me = lax.axis_index("tile")
@@ -40,6 +40,12 @@
             src_ref=src, dst_ref=dst, send_sem=send_sem, recv_sem=recv_sem, device_id=device, device_id_type=MESH
         )
 
+    mine = pl.ds(pl.multiple_of(core * HALF, HALF), HALF)
+    load_innov = pltpu.make_async_copy(innov_hbm, innov_ref, load_sem.at[0])
+    load_a = pltpu.make_async_copy(a_ref, a_win.at[TILES : 2 * TILES, mine], load_sem.at[1])
+    load_innov.start()
+    load_a.start()
+
     not_first, not_last = me > 0, me < size - 1
     to_side, from_side = (not_last, not_first), (not_first, not_last)
 
@@ -60,7 +66,6 @@
     def _():
         pl.semaphore_wait(barrier, 2)
 
-    mine = pl.ds(pl.multiple_of(core * HALF, HALF), HALF)
     a_out = [[], [], []]
     for t in range(TILES):
         for side, (device, slot) in enumerate(((right, t), (left, 2 * TILES + t), (sibling, TILES + t))):
@@ -87,8 +92,8 @@
         from_left[...] = jnp.zeros_like(from_left)
         for n in range(SLOTS):
             before_bin[n] = NBIN
-            before_pair[n, 0] = 0
-            before_pair[n, 1] = 0
+            before_pair[0, n] = 0
+            before_pair[1, n] = 0
 
     @pl.when(me == size - 1)
     def _():
@@ -97,6 +102,7 @@
             g_win[h][2 * TILES :] = jnp.zeros((TILES, ROWS, POINTS), jnp.bfloat16)
         from_right[...] = jnp.zeros_like(from_right)
 
+    load_innov.wait()
     base = me * TILES
     g_out = [[], []]
     for h in range(CHUNKS):
@@ -110,10 +116,6 @@
         for side, (device, slot) in enumerate(((right, 0), (left, 2 * TILES))):
             there = g_win[h].at[slot : slot + TILES]
             g_out[side].append(send(here, there, g_send.at[side, h], g_recv.at[side, h], device))
-            pl.when(to_side[side])(g_out[side][h].start)
-
-    for t in range(TILES):
-        a_win[TILES + t, mine] = a_ref[t]
 
     def weigh(n, _):
         b = n // (POINTS // BAND)
@@ -128,12 +130,16 @@
 
     lax.fori_loop(0, NBIN * (POINTS // BAND), weigh, 0)
 
-    def product(turned, second, weights_of, target):
+    def product(turned, second, weights_of, target, also_turned=None):
         for band in range(POINTS // BAND):
             rows = slice(band * BAND, (band + 1) * BAND)
             cross = jnp.dot(turned(rows), second, preferred_element_type=jnp.float32)
-            target[rows, :] = (weights_of(rows) * cross).astype(jnp.bfloat16)
-
+            rounded = (weights_of(rows) * cross).astype(jnp.bfloat16)
+            target[rows, :] = rounded
+            if also_turned is not None:
+                also_turned[:, rows] = rounded.T
+
+    load_a.wait()
     for t in range(TILES):
         a_out[2][t].wait_recv()
 
@@ -156,6 +162,11 @@
                 a_out[side][t].wait_recv()
                 relays[side][t].start()
 
+        for h, when in enumerate((2, 3)):
+            if when == t:
+                for side in range(2):
+                    pl.when(to_side[side])(g_out[side][h].start)
+
     @pl.when(not_first)
     def _():
         for copy in info_out + relays[0]:
@@ -176,8 +187,8 @@
     shift = base - TILES
 
     def slot_of(n):
-        own = (pair_ref[n, 0] - shift, pair_ref[n, 1] - shift, bin_ref[n])
-        far = (before_pair[n, 0] - base_before, before_pair[n, 1] - base_before, before_bin[n])
+        own = (pair_ref[0, n] - shift, pair_ref[1, n] - shift, bin_ref[n])
+        far = (before_pair[0, n] - base_before, before_pair[1, n] - base_before, before_bin[n])
         return own, far
 
     def inside(first, second, b):
@@ -187,15 +198,21 @@
         for k, ends in enumerate(slot_of(n)):
             first, second, b = inside(*ends)
             product(
-                lambda rows: a_turned[first, rows, :], a_win[second], lambda rows: rho[b, rows, :], cov.at[k * SLOTS + n]
+                lambda rows: a_turned[first, rows, :], a_win[second], lambda rows: rho[b, rows, :], cov.at[k * SLOTS + n],
+                cov_turned.at[k * SLOTS + n],
             )
         return 0
 
     lax.fori_loop(0, SLOTS, covariance, 0)
 
     i_out = [[], []]
-    nn = (((1,), (0,)), ((), ()))
-    nt = (((1,), (1,)), ((), ()))
+    slots = [slot_of(n) for n in range(SLOTS)]
+
+    def hit(end, tile, bin_, alive):
+        return jnp.where((end == tile) & (bin_ < NBIN) & alive, 1.0, 0.0).astype(jnp.float32)
+
+    near = [pair_ref[1, n] - base < 2 * TILES for n in range(SLOTS)]
+    away = [before_pair[1, n] - base_before >= 2 * TILES for n in range(SLOTS)]
     for h in range(CHUNKS):
         for side in range(2):
             pl.when(from_side[side])(g_out[side][h].wait_recv)
@@ -203,44 +220,35 @@
         def increments(n, _):
             for k, ends in enumerate(slot_of(n)):
                 first, second, _ = inside(*ends)
-                matrix = cov[k * SLOTS + n]
-                to_first[k * SLOTS + n] = lax.dot_general(
-                    g_win[h][second], matrix, nt, preferred_element_type=jnp.float32
-                )
-                to_second[k * SLOTS + n] = lax.dot_general(
-                    g_win[h][first], matrix, nn, preferred_element_type=jnp.float32
-                )
+                u = k * SLOTS + n
+                to_first[h, u] = jnp.dot(g_win[h][second], cov_turned[u], preferred_element_type=jnp.float32)
+                to_second[h, u] = jnp.dot(g_win[h][first], cov[u], preferred_element_type=jnp.float32)
             return 0
 
         lax.fori_loop(0, SLOTS, increments, 0)
 
-        slots = [slot_of(n) for n in range(SLOTS)]
-
-        def hit(end, tile, bin_, alive):
-            return jnp.where((end == tile) & (bin_ < NBIN) & alive, 1.0, 0.0).astype(jnp.float32)
-
-        near = [pair_ref[n, 1] - base < 2 * TILES for n in range(SLOTS)]
-        away = [before_pair[n, 1] - base_before >= 2 * TILES for n in range(SLOTS)]
         for t in range(TILES):
             total = jnp.zeros((ROWS, POINTS), jnp.float32)
             for n, (_, (first, _, b)) in enumerate(slots):
-                total = total + hit(first, t, b, away[n]) * to_first[SLOTS + n]
+                total = total + hit(first, t, b, away[n]) * to_first[h, SLOTS + n]
             i_left[h, t] = total.astype(jnp.bfloat16)
             total = jnp.zeros((ROWS, POINTS), jnp.float32)
             for n, ((_, second, b), (_, far_second, far_b)) in enumerate(slots):
-                total = total + hit(second, 2 * TILES + t, b, near[n]) * to_second[n]
-                total = total + hit(far_second, 2 * TILES + t, far_b, away[n]) * to_second[SLOTS + n]
+                total = total + hit(second, 2 * TILES + t, b, near[n]) * to_second[h, n]
+                total = total + hit(far_second, 2 * TILES + t, far_b, away[n]) * to_second[h, SLOTS + n]
             i_right[h, t] = total.astype(jnp.bfloat16)
         for side, (device, src, dst) in enumerate(((right, i_right, from_left), (left, i_left, from_right))):
             i_out[side].append(send(src.at[h], dst.at[h], i_send.at[side, h], i_recv.at[side, h], device))
             pl.when(to_side[side])(i_out[side][h].start)
+
+    for h in range(CHUNKS):
+        rows = pl.ds(pl.multiple_of(core * HALF + h * ROWS, ROWS), ROWS)
         for t in range(TILES):
-            rows = slice(h * ROWS, (h + 1) * ROWS)
             total = jnp.dot(g_win[h][TILES + t], own_cov[t], preferred_element_type=jnp.float32)
-            total = total + a_ref[t, rows, :].astype(jnp.float32)
+            total = total + a_win[TILES + t, rows, :].astype(jnp.float32)
             for n, ((first, second, b), _) in enumerate(slots):
-                total = total + hit(first, TILES + t, b, near[n]) * to_first[n]
-                total = total + hit(second, TILES + t, b, near[n]) * to_second[n]
+                total = total + hit(first, TILES + t, b, near[n]) * to_first[h, n]
+                total = total + hit(second, TILES + t, b, near[n]) * to_second[h, n]
             own_total[h, t] = total
 
     for h in range(CHUNKS):
@@ -270,18 +278,26 @@
             copy.wait_send()
 
 
+def hand_on(src, dst, sem):
+    copy = pltpu.make_async_copy(src, dst, sem)
+    copy.start()
+    copy.wait()
+
+
 def per_device(anomalies, innovations, obs_tile, pair_tiles, loc_bin):
     bf16, f32 = jnp.bfloat16, jnp.float32
     vmem, smem = pl.BlockSpec(memory_space=pltpu.VMEM), pl.BlockSpec(memory_space=pltpu.SMEM)
+    hbm = pl.BlockSpec(memory_space=pl.ANY)
     dma = pltpu.SemaphoreType.DMA
-    return pl.pallas_call(
+    made = pl.pallas_call(
         kernel,
         name="analysis",
-        out_shape=jax.ShapeDtypeStruct(anomalies.shape, bf16),
-        in_specs=[smem, smem, smem, vmem, vmem],
+        out_shape=pltpu.VMEM(anomalies.shape, bf16),
+        in_specs=[smem, smem, smem, hbm, hbm],
         out_specs=vmem,
         scratch_shapes=[
-            pltpu.SMEM((SLOTS, 2), jnp.int32),
+            pltpu.VMEM(innovations.shape, bf16),
+            pltpu.SMEM((2, SLOTS), jnp.int32),
             pltpu.SMEM((SLOTS,), jnp.int32),
             pltpu.VMEM((3 * TILES, MEMBERS, POINTS), bf16),
             pltpu.VMEM((2 * TILES, POINTS, MEMBERS), bf16),
@@ -289,9 +305,10 @@
             pltpu.VMEM((3 * TILES, ROWS, POINTS), bf16),
             pltpu.VMEM((NBIN, POINTS, POINTS), f32),
             pltpu.VMEM((2 * SLOTS, POINTS, POINTS), bf16),
+            pltpu.VMEM((2 * SLOTS, POINTS, POINTS), bf16),
             pltpu.VMEM((TILES, POINTS, POINTS), bf16),
-            pltpu.VMEM((2 * SLOTS, ROWS, POINTS), f32),
-            pltpu.VMEM((2 * SLOTS, ROWS, POINTS), f32),
+            pltpu.VMEM((CHUNKS, 2 * SLOTS, ROWS, POINTS), f32),
+            pltpu.VMEM((CHUNKS, 2 * SLOTS, ROWS, POINTS), f32),
             pltpu.VMEM((CHUNKS, TILES, ROWS, POINTS), bf16),
             pltpu.VMEM((CHUNKS, TILES, ROWS, POINTS), bf16),
             pltpu.VMEM((CHUNKS, TILES, ROWS, POINTS), bf16),
@@ -301,10 +318,18 @@
             dma((2, TILES)), dma((2, TILES)),
             dma((2, CHUNKS)), dma((2, CHUNKS)),
             dma((2, CHUNKS)), dma((2, CHUNKS)),
-            dma((2,)), dma((2,)),
+            dma((2,)), dma((2,)), dma((2,)),
         ],
         compiler_params=pltpu.CompilerParams(collective_id=0, has_side_effects=True, vmem_limit_bytes=56 << 20),
-    )(obs_tile, pair_tiles, loc_bin, anomalies, innovations)
+    )(obs_tile, pair_tiles.T, loc_bin, anomalies, innovations)
+    return pl.pallas_call(
+        hand_on,
+        name="hand_on",
+        out_shape=jax.ShapeDtypeStruct(anomalies.shape, bf16),
+        in_specs=[vmem],
+        out_specs=hbm,
+        scratch_shapes=[pltpu.SemaphoreType.DMA],
+    )(pltpu.with_memory_space_constraint(made, pltpu.VMEM))
 
 
 def solution(mesh):

time: 56.9 us -> 51 us (0.90)
  local copies, waits for them, and re-layouts: 3.21 us -> 0 us
  Pallas kernels: 53.1 us -> 50.7 us
    unnamed x2 -> x0, local copies, waits for them, and re-layouts: 3.21 us -> none
    pallas_call x1 -> x2, Pallas kernels: 53.1 us -> 50.7 us  [the longest x1 49.9 us: per_device(): pl.pallas_call(kernel, name='analysis', out_shape=pltpu.VMEM(anomalies.sh...]
where the time goes in v3:
time: 51 us; the launch traced here: 50.7 us
  Pallas kernels  50.7 us (99%)
    pallas_call x1, Pallas kernels, per_device(): pl.pallas_call(kernel, name='analysis', out_shape=pltpu.VMEM(anomalies.sh...  49.9 us

profile of v3, /device:TPU:448, one launch (start us, length us, event | category | flops | bytes accessed | tf_op | source)
XLA Modules:
  0.0 50.7 jit_solution(11896406804811222426)
XLA Ops:
  0.0 49.9 %analysis.1.src = bf16[4,128,512]{2,1,0:T(8,128)(2,1)S(1)} custom-call(s32[8]{0:T(128)} %obs_ref.1, s32[2,8]{1,0:T(2,128)} %bitcast.1, s32[8]{0:T(128)} %bin_ref.1, bf16[4,128,512]{2,1,0:T(8,128)(2,1)} %a_ref.1, bf16[8,128,512]{2,1,0:T(8,128)(2,1)} %innov_hbm.1), custom_call_target="tpu_custom_call" | custom-call | tf_op jit(solution)/shard_map/analysis/pallas_call | solution.py:292
  49.9 0.8 %hand_on.1 = bf16[4,128,512]{2,1,0:T(8,128)(2,1)} custom-call(bf16[4,128,512]{2,1,0:T(8,128)(2,1)S(1)} %analysis.1.src), custom_call_target="tpu_custom_call" | custom-call | tf_op jit(solution)/shard_map/hand_on/pallas_call | solution.py:325

commit v4 on v3

v4 whole, which is shorter than its diff:
```python
import functools

import jax
import jax.numpy as jnp
from jax import lax
from jax.experimental import pallas as pl
from jax.experimental.pallas import tpu as pltpu
from jax.sharding import PartitionSpec as P

MEMBERS = 256
POINTS = 512
NBIN = 4
RADIUS = 4
TILES = 4
SLOTS = 8
BLOCKS = 8
HALF = MEMBERS // 2
CHUNKS = 2
ROWS = HALF // CHUNKS
BAND = 128
UNROLL = 2
TALL = 256
MESH = pl.DeviceIdType.MESH


def kernel(
    obs_ref, pair_ref, bin_ref, a_ref, innov_hbm, out_ref,
    innov_ref, before_pair, before_bin, a_left, a_near, a_turned, g_own, g_left0, g_left1, g_near0, g_near1,
    rho, cov, cov_turned, own_cov, near_second, far_first, far_second,
    right_sum, own_sum, i_left, i_right, from_left, from_right,
    a_send, a_recv, relay_send, relay_recv, g_send, g_recv, i_send, i_recv, info_send, info_recv, load_sem,
):
    core = lax.axis_index("mem")
    me = lax.axis_index("tile")
    size = lax.axis_size("tile")
    right = (core, lax.rem(me + 1, size))
    left = (core, lax.rem(me + size - 1, size))
    sibling = (1 - core, me)
    g_left, g_near = (g_left0, g_left1), (g_near0, g_near1)

    def send(src, dst, send_sem, recv_sem, device):
        return pltpu.make_async_remote_copy(
            src_ref=src, dst_ref=dst, send_sem=send_sem, recv_sem=recv_sem, device_id=device, device_id_type=MESH
        )

    mine = pl.ds(pl.multiple_of(core * HALF, HALF), HALF)
    load_innov = pltpu.make_async_copy(innov_hbm, innov_ref, load_sem.at[0])
    load_a = pltpu.make_async_copy(a_ref, a_near.at[:TILES, mine], load_sem.at[1])
    load_innov.start()
    load_a.start()

    not_first, not_last = me > 0, me < size - 1
    to_side, from_side = (not_last, not_first), (not_first, not_last)

    barrier = pltpu.get_barrier_semaphore()
    for device, there in ((left, not_first), (right, not_last), (sibling, None)):

        def greet():
            pl.semaphore_signal(barrier, inc=1, device_id=device, device_id_type=MESH)

        greet() if there is None else pl.when(there)(greet)
    both = not_first & not_last

    @pl.when(both)
    def _():
        pl.semaphore_wait(barrier, 3)

    @pl.when(jnp.logical_not(both))
    def _():
        pl.semaphore_wait(barrier, 2)

    a_out = [[], [], []]
    for t in range(TILES):
        for side, (device, there) in enumerate(
            ((right, a_left.at[t, mine]), (left, a_near.at[TILES + t, mine]), (sibling, a_near.at[t, mine]))
        ):
            a_out[side].append(send(a_ref.at[t], there, a_send.at[side, t], a_recv.at[side, t], device))
    info_out = [
        send(pair_ref, before_pair, info_send.at[0], info_recv.at[0], right),
        send(bin_ref, before_bin, info_send.at[1], info_recv.at[1], right),
    ]
    for t in range(TILES):
        for side in range(2):
            pl.when(to_side[side])(a_out[side][t].start)
        a_out[2][t].start()

    @pl.when(not_last)
    def _():
        for copy in info_out:
            copy.start()

    @pl.when(me == 0)
    def _():
        a_left[...] = jnp.zeros_like(a_left)
        from_left[...] = jnp.zeros_like(from_left)
        for h in range(CHUNKS):
            g_left[h][...] = jnp.zeros_like(g_left[h])
        for n in range(SLOTS):
            before_bin[n] = NBIN
            before_pair[0, n] = 0
            before_pair[1, n] = 0

    @pl.when(me == size - 1)
    def _():
        a_near[TILES:] = jnp.zeros((TILES, MEMBERS, POINTS), jnp.bfloat16)
        from_right[...] = jnp.zeros_like(from_right)
        for h in range(CHUNKS):
            g_near[h][TILES:] = jnp.zeros((TILES, ROWS, POINTS), jnp.bfloat16)

    load_innov.wait()
    base = me * TILES
    g_out = [[], []]
    for h in range(CHUNKS):
        rows = slice(h * ROWS, (h + 1) * ROWS)
        for t in range(TILES):
            total = jnp.zeros((ROWS, POINTS), jnp.float32)
            for o in range(BLOCKS):
                share = jnp.where(obs_ref[o] - base == t, 1.0, 0.0).astype(jnp.float32)
                total = total + share * innov_ref[o, rows, :].astype(jnp.float32)
            g_own[t, rows, :] = total.astype(jnp.bfloat16)
            g_near[h][t] = total.astype(jnp.bfloat16)
        here = g_own.at[:, rows]
        for side, (device, there) in enumerate(((right, g_left[h]), (left, g_near[h].at[TILES:]))):
            g_out[side].append(send(here, there, g_send.at[side, h], g_recv.at[side, h], device))

    def weigh(n, _):
        b = n // (POINTS // BAND)
        start = pl.multiple_of(lax.rem(n, POINTS // BAND) * BAND, BAND)
        p = lax.broadcasted_iota(jnp.int32, (BAND, POINTS), 0) + start
        q = lax.broadcasted_iota(jnp.int32, (BAND, POINTS), 1)
        along = ((q & 31) - (p & 31)).astype(jnp.float32) + 0.5 * RADIUS * b.astype(jnp.float32)
        across = ((q >> 5) - (p >> 5)).astype(jnp.float32)
        weight = jnp.exp(-(along * along + across * across) / (2.0 * RADIUS * RADIUS))
        rho[b, pl.ds(start, BAND), :] = weight * (1.0 / (MEMBERS - 1))
        return 0

    lax.fori_loop(0, NBIN * (POINTS // BAND), weigh, 0)

    def product(turned, second, weights_of, target, also_turned=None):
        for band in range(POINTS // TALL):
            rows = slice(band * TALL, (band + 1) * TALL)
            cross = jnp.dot(turned(rows), second, preferred_element_type=jnp.float32)
            rounded = (weights_of(rows) * cross).astype(jnp.bfloat16)
            target[rows, :] = rounded
            if also_turned is not None:
                also_turned[:, rows] = rounded.T

    load_a.wait()
    for t in range(TILES):
        a_out[2][t].wait_recv()

    def own_product(t, _):
        tile = a_near[t]
        a_turned[TILES + t] = tile.T
        product(lambda rows: a_turned[TILES + t, rows, :], tile, lambda rows: rho[0, rows, :], own_cov.at[t])
        return 0

    lax.fori_loop(0, TILES, own_product, 0)

    relays = [[], []]
    for t in range(TILES):
        for side, here in ((0, a_left.at[t, mine]), (1, a_near.at[TILES + t, mine])):
            relays[side].append(send(here, here, relay_send.at[side, t], relay_recv.at[side, t], sibling))

            @pl.when(from_side[side])
            def _():
                a_out[side][t].wait_recv()
                relays[side][t].start()

        if t == TILES - 2:
            for side in range(2):
                pl.when(to_side[side])(g_out[side][0].start)


    @pl.when(not_last)
    def _():
        for copy in relays[1]:
            copy.wait_recv()

    for side in range(2):
        pl.when(to_side[side])(g_out[side][1].start)

    near = [(pair_ref[0, n] - base, pair_ref[1, n] - base, bin_ref[n]) for n in range(SLOTS)]

    def near_covariance(n, _):
        first = jnp.clip(pair_ref[0, n] - base, 0, TILES - 1)
        second = jnp.clip(pair_ref[1, n] - base, 0, 2 * TILES - 1)
        b = jnp.clip(bin_ref[n], 0, NBIN - 1)
        product(
            lambda rows: a_turned[TILES + first, rows, :], a_near[second], lambda rows: rho[b, rows, :], cov.at[n],
            cov_turned.at[n],
        )
        return 0


    @pl.when(not_first)
    def _():
        for copy in info_out + relays[0]:
            copy.wait_recv()

    base_before = lax.rem(me + size - 1, size) * TILES
    far = [(before_pair[0, n] - base_before, before_pair[1, n] - base_before, before_bin[n]) for n in range(SLOTS)]

    def turn(t, _):
        a_turned[t] = a_left[t].T
        return 0

    lax.fori_loop(0, TILES, turn, 0)

    def far_ends(n):
        first = jnp.clip(before_pair[0, n] - base_before, 0, TILES - 1)
        second = jnp.clip(before_pair[1, n] - base_before - TILES, TILES, 2 * TILES - 1)
        return first, second

    def far_covariance(n, _):
        first, second = far_ends(n)
        b = jnp.clip(before_bin[n], 0, NBIN - 1)
        product(
            lambda rows: a_turned[first, rows, :], a_near[second], lambda rows: rho[b, rows, :], cov.at[SLOTS + n],
            cov_turned.at[SLOTS + n],
        )
        return 0

    def covariances(n, _):
        near_covariance(n, 0)
        far_covariance(n, 0)
        return 0

    lax.fori_loop(0, SLOTS, covariances, 0, unroll=UNROLL)

    def near_seconds(n, _):
        first = jnp.clip(pair_ref[0, n] - base, 0, TILES - 1)
        near_second[n] = jnp.dot(g_own[first], cov[n], preferred_element_type=jnp.float32)
        return 0

    lax.fori_loop(0, SLOTS, near_seconds, 0, unroll=4)

    def share_of(alive, end, tile, b):
        return jnp.where(alive & (end == tile) & (b < NBIN), 1.0, 0.0).astype(jnp.float32)

    for h in range(CHUNKS):
        rows = slice(h * ROWS, (h + 1) * ROWS)
        for t in range(TILES):
            total = jnp.zeros((ROWS, POINTS), jnp.float32)
            for n, (_, second, b) in enumerate(near):
                total = total + share_of(second < 2 * TILES, second, TILES + t, b) * near_second[n, rows, :]
            right_sum[t, rows, :] = total

    i_out = [[], []]
    for h in range(CHUNKS):
        rows = slice(h * ROWS, (h + 1) * ROWS)
        for side in range(2):
            pl.when(from_side[side])(g_out[side][h].wait_recv)

        def increments(n, _):
            first, second = far_ends(n)
            far_first[n] = jnp.dot(g_near[h][second], cov_turned[SLOTS + n], preferred_element_type=jnp.float32)
            far_second[n] = jnp.dot(g_left[h][first], cov[SLOTS + n], preferred_element_type=jnp.float32)
            return 0

        lax.fori_loop(0, SLOTS, increments, 0, unroll=4)
        for t in range(TILES):
            to_left = jnp.zeros((ROWS, POINTS), jnp.float32)
            to_right = right_sum[t, rows, :]
            for n, (first, second, b) in enumerate(far):
                alive = second >= 2 * TILES
                to_left = to_left + share_of(alive, first, t, b) * far_first[n]
                to_right = to_right + share_of(alive, second, 2 * TILES + t, b) * far_second[n]
            i_left[h, t] = to_left.astype(jnp.bfloat16)
            i_right[h, t] = to_right.astype(jnp.bfloat16)
        for side, (device, src, dst) in enumerate(((right, i_right, from_left), (left, i_left, from_right))):
            i_out[side].append(send(src.at[h], dst.at[h], i_send.at[side, h], i_recv.at[side, h], device))
            pl.when(to_side[side])(i_out[side][h].start)

    for t in range(TILES):
        total = jnp.dot(g_own[t], own_cov[t], preferred_element_type=jnp.float32)
        own_sum[t] = total + a_near[t, mine, :].astype(jnp.float32)

    def near_increment(n, _):
        first = jnp.clip(pair_ref[0, n] - base, 0, TILES - 1)
        second = jnp.clip(pair_ref[1, n] - base, 0, 2 * TILES - 1)
        alive = (pair_ref[1, n] - base < 2 * TILES) & (bin_ref[n] < NBIN)
        forcing = jnp.concatenate([g_near[h][second] for h in range(CHUNKS)], axis=0)
        to_first = jnp.dot(forcing, cov_turned[n], preferred_element_type=jnp.float32)
        for t in range(TILES):
            share_first = jnp.where(alive & (first == t), 1.0, 0.0).astype(jnp.float32)
            share_second = jnp.where(alive & (second == t), 1.0, 0.0).astype(jnp.float32)
            own_sum[t] = own_sum[t] + (share_first * to_first + share_second * near_second[n])
        return 0

    lax.fori_loop(0, SLOTS, near_increment, 0)

    for h in range(CHUNKS):
        rows = slice(h * ROWS, (h + 1) * ROWS)
        for side in range(2):
            pl.when(from_side[side])(i_out[side][h].wait_recv)
        for t in range(TILES):
            total = own_sum[t, rows, :] + from_left[h, t].astype(jnp.float32) + from_right[h, t].astype(jnp.float32)
            out_ref[t, rows, :] = total.astype(jnp.bfloat16)

    for copy in a_out[2]:
        copy.wait_send()
    for side in range(2):

        @pl.when(to_side[side])
        def _():
            for copy in a_out[side] + g_out[side] + i_out[side]:
                copy.wait_send()

        @pl.when(from_side[side])
        def _():
            for copy in relays[side]:
                copy.wait_send()

    @pl.when(not_last)
    def _():
        for copy in info_out:
            copy.wait_send()


def hand_on(src, dst, sem):
    copy = pltpu.make_async_copy(src, dst, sem)
    copy.start()
    copy.wait()


def per_device(anomalies, innovations, obs_tile, pair_tiles, loc_bin):
    bf16, f32 = jnp.bfloat16, jnp.float32
    vmem, smem = pl.BlockSpec(memory_space=pltpu.VMEM), pl.BlockSpec(memory_space=pltpu.SMEM)
    hbm = pl.BlockSpec(memory_space=pl.ANY)
    dma = pltpu.SemaphoreType.DMA
    made = pl.pallas_call(
        kernel,
        name="analysis",
        out_shape=pltpu.VMEM(anomalies.shape, bf16),
        in_specs=[smem, smem, smem, hbm, hbm],
        out_specs=vmem,
        scratch_shapes=[
            pltpu.VMEM(innovations.shape, bf16),
            pltpu.SMEM((2, SLOTS), jnp.int32),
            pltpu.SMEM((SLOTS,), jnp.int32),
            pltpu.VMEM((TILES, MEMBERS, POINTS), bf16),
            pltpu.VMEM((2 * TILES, MEMBERS, POINTS), bf16),
            pltpu.VMEM((2 * TILES, POINTS, MEMBERS), bf16),
            pltpu.VMEM((TILES, HALF, POINTS), bf16),
            pltpu.VMEM((TILES, ROWS, POINTS), bf16),
            pltpu.VMEM((TILES, ROWS, POINTS), bf16),
            pltpu.VMEM((2 * TILES, ROWS, POINTS), bf16),
            pltpu.VMEM((2 * TILES, ROWS, POINTS), bf16),
            pltpu.VMEM((NBIN, POINTS, POINTS), f32),
            pltpu.VMEM((2 * SLOTS, POINTS, POINTS), bf16),
            pltpu.VMEM((2 * SLOTS, POINTS, POINTS), bf16),
            pltpu.VMEM((TILES, POINTS, POINTS), bf16),
            pltpu.VMEM((SLOTS, HALF, POINTS), f32),
            pltpu.VMEM((SLOTS, ROWS, POINTS), f32),
            pltpu.VMEM((SLOTS, ROWS, POINTS), f32),
            pltpu.VMEM((TILES, HALF, POINTS), f32),
            pltpu.VMEM((TILES, HALF, POINTS), f32),
            pltpu.VMEM((CHUNKS, TILES, ROWS, POINTS), bf16),
            pltpu.VMEM((CHUNKS, TILES, ROWS, POINTS), bf16),
            pltpu.VMEM((CHUNKS, TILES, ROWS, POINTS), bf16),
            pltpu.VMEM((CHUNKS, TILES, ROWS, POINTS), bf16),
            dma((3, TILES)), dma((3, TILES)),
            dma((2, TILES)), dma((2, TILES)),
            dma((2, CHUNKS)), dma((2, CHUNKS)),
            dma((2, CHUNKS)), dma((2, CHUNKS)),
            dma((2,)), dma((2,)), dma((2,)),
        ],
        compiler_params=pltpu.CompilerParams(collective_id=0, has_side_effects=True, vmem_limit_bytes=56 << 20),
    )(obs_tile, pair_tiles.T, loc_bin, anomalies, innovations)
    return pl.pallas_call(
        hand_on,
        name="hand_on",
        out_shape=jax.ShapeDtypeStruct(anomalies.shape, bf16),
        in_specs=[vmem],
        out_specs=hbm,
        scratch_shapes=[pltpu.SemaphoreType.DMA],
    )(pltpu.with_memory_space_constraint(made, pltpu.VMEM))


def solution(mesh):
    return jax.shard_map(
        per_device,
        mesh=mesh,
        in_specs=(
            P("tile", "mem", None),
            P("tile", "mem", None),
            P("tile"),
            P("tile", None),
            P("tile"),
        ),
        out_specs=P("tile", "mem", None),
        check_vma=False,
    )
```

time: 51 us -> 48.7 us (0.955)
  Pallas kernels: 50.7 us -> 48.2 us
    pallas_call x1, Pallas kernels: 49.9 us -> 47.4 us  [per_device(): pl.pallas_call(kernel, name='analysis', out_shape=pltpu.VMEM(anomalies.sh...]
where the time goes in v4:
time: 48.7 us; the launch traced here: 48.2 us
  Pallas kernels  48.2 us (99%)
    pallas_call x1, Pallas kernels, per_device(): pl.pallas_call(kernel, name='analysis', out_shape=pltpu.VMEM(anomalies.sh...  47.4 us

profile of v4, /device:TPU:448, one launch (start us, length us, event | category | flops | bytes accessed | tf_op | source)
XLA Modules:
  0.0 48.2 jit_solution(13127896635931882796)
XLA Ops:
  0.0 47.4 %analysis.1.src = bf16[4,128,512]{2,1,0:T(8,128)(2,1)S(1)} custom-call(s32[8]{0:T(128)} %obs_ref.1, s32[2,8]{1,0:T(2,128)} %bitcast.1, s32[8]{0:T(128)} %bin_ref.1, bf16[4,128,512]{2,1,0:T(8,128)(2,1)} %a_ref.1, bf16[8,128,512]{2,1,0:T(8,128)(2,1)} %innov_hbm.1), custom_call_target="tpu_custom_call" | custom-call | tf_op jit(solution)/shard_map/analysis/pallas_call | solution.py:332
  47.4 0.8 %hand_on.1 = bf16[4,128,512]{2,1,0:T(8,128)(2,1)} custom-call(bf16[4,128,512]{2,1,0:T(8,128)(2,1)S(1)} %analysis.1.src), custom_call_target="tpu_custom_call" | custom-call | tf_op jit(solution)/shard_map/hand_on/pallas_call | solution.py:371

commit v5 on v4

--- a/solution.py
+++ b/solution.py
@@ -18,7 +18,7 @@
 CHUNKS = 2
 ROWS = HALF // CHUNKS
 BAND = 128
-UNROLL = 2
+UNROLL = 4
 TALL = 256
 MESH = pl.DeviceIdType.MESH
 
@@ -167,18 +167,15 @@
                 a_out[side][t].wait_recv()
                 relays[side][t].start()
 
-        if t == TILES - 2:
+        if t >= TILES - 2:
             for side in range(2):
-                pl.when(to_side[side])(g_out[side][0].start)
+                pl.when(to_side[side])(g_out[side][t - TILES + 2].start)
 
 
     @pl.when(not_last)
     def _():
         for copy in relays[1]:
             copy.wait_recv()
-
-    for side in range(2):
-        pl.when(to_side[side])(g_out[side][1].start)
 
     near = [(pair_ref[0, n] - base, pair_ref[1, n] - base, bin_ref[n]) for n in range(SLOTS)]
 
@@ -205,7 +202,7 @@
         a_turned[t] = a_left[t].T
         return 0
 
-    lax.fori_loop(0, TILES, turn, 0)
+    lax.fori_loop(0, TILES, turn, 0, unroll=4)
 
     def far_ends(n):
         first = jnp.clip(before_pair[0, n] - base_before, 0, TILES - 1)
@@ -233,7 +230,7 @@
         near_second[n] = jnp.dot(g_own[first], cov[n], preferred_element_type=jnp.float32)
         return 0
 
-    lax.fori_loop(0, SLOTS, near_seconds, 0, unroll=4)
+    lax.fori_loop(0, SLOTS, near_seconds, 0, unroll=8)
 
     def share_of(alive, end, tile, b):
         return jnp.where(alive & (end == tile) & (b < NBIN), 1.0, 0.0).astype(jnp.float32)
@@ -258,7 +255,7 @@
             far_second[n] = jnp.dot(g_left[h][first], cov[SLOTS + n], preferred_element_type=jnp.float32)
             return 0
 
-        lax.fori_loop(0, SLOTS, increments, 0, unroll=4)
+        lax.fori_loop(0, SLOTS, increments, 0, unroll=8)
         for t in range(TILES):
             to_left = jnp.zeros((ROWS, POINTS), jnp.float32)
             to_right = right_sum[t, rows, :]

time: 48.7 us -> 47.2 us (0.969)
  Pallas kernels: 48.2 us -> 47.1 us
    pallas_call x1, Pallas kernels: 47.4 us -> 46.2 us  [per_device(): pl.pallas_call(kernel, name='analysis', out_shape=pltpu.VMEM(anomalies.sh...]
where the time goes in v5:
time: 47.2 us; the launch traced here: 47.1 us
  Pallas kernels  47.1 us (100%)
    pallas_call x1, Pallas kernels, per_device(): pl.pallas_call(kernel, name='analysis', out_shape=pltpu.VMEM(anomalies.sh...  46.2 us

profile of v5, /device:TPU:448, one launch (start us, length us, event | category | flops | bytes accessed | tf_op | source)
XLA Modules:
  0.0 47.1 jit_solution(5216775226529025726)
XLA Ops:
  0.0 46.2 %analysis.1.src = bf16[4,128,512]{2,1,0:T(8,128)(2,1)S(1)} custom-call(s32[8]{0:T(128)} %obs_ref.1, s32[2,8]{1,0:T(2,128)} %bitcast.1, s32[8]{0:T(128)} %bin_ref.1, bf16[4,128,512]{2,1,0:T(8,128)(2,1)} %a_ref.1, bf16[8,128,512]{2,1,0:T(8,128)(2,1)} %innov_hbm.1), custom_call_target="tpu_custom_call" | custom-call | tf_op jit(solution)/shard_map/analysis/pallas_call | solution.py:329
  46.3 0.8 %hand_on.1 = bf16[4,128,512]{2,1,0:T(8,128)(2,1)} custom-call(bf16[4,128,512]{2,1,0:T(8,128)(2,1)S(1)} %analysis.1.src), custom_call_target="tpu_custom_call" | custom-call | tf_op jit(solution)/shard_map/hand_on/pallas_call | solution.py:368
